TPU v7x, 256 devices: a whole 4x4x8 slice. The times are simulated.
256 devices in a mesh: shell: 4 (over z_hi, core), blk: 64 (over z_lo, y, x).
Axes of the slice: x: 4, y: 4, z: 8 (z_hi: 2, z_lo: 4; z = z_hi * 4 + z_lo), core: 2. Of those that a mesh axis runs over, the one named last changes fastest.
Arguments:
- strain_spec: bfloat16 [6, 4, 1024, 2, 1024], P(None, 'shell', 'blk'), may hold values from -6 to 6
- order_map: int32 [1024], replicated, may hold values from 0 to 1023, as said below
- viscosity: float32 [4, 1024, 2048], P('shell', 'blk'), may hold values from 0.2 to 5
- radial_weight: float32 [4], P('shell'), may hold values from 0.3 to 3
Outputs:
- stress_spec: bfloat16 [6, 4, 1024, 2, 1024], P(None, 'shell', 'blk')
- integrated: float32 [6, 1024, 2, 1024], P(None, 'blk', None, 'shell')
Inputs may be any that keep to these rules, and one draw needn't show every extreme that they name: order_map is a permutation of the orders 0 to 1023; the entries 2i and 2i + 1 hold two orders m and 1023 - m, in either order, so each device's 16 slots hold 8 such pairs.
All inputs are finite; a program needn't handle non-finite values.
Results may differ from a plain program's by a relative error of at most 0.014.
Values may be sent and summed in bfloat16 or wider, within the bound.
A program may use at most 128 MiB of HBM per device.

v0:
```python
import math
import jax
import jax.numpy as jnp
from jax import lax
from jax.sharding import PartitionSpec as P

two_power = 1099511627776.0
inverse_power = 1.0 / 1099511627776.0
log_jump = 40.0 * math.log(2.0)


def cycle_geometry(cycle_count):
    cycle_index = jnp.arange(cycle_count // 2, dtype=jnp.float32)
    colatitude = math.pi * (2.0 * cycle_index + 1.0) / (2.0 * cycle_count)
    return (jnp.cos(colatitude), jnp.log(jnp.sin(colatitude)))


def fejer_weights(cycle_count):
    half_count = cycle_count // 2
    cycle_index = jnp.arange(half_count, dtype=jnp.int32)
    wave_number = jnp.arange(1, half_count + 1, dtype=jnp.int32)
    phase_index = wave_number[:, None] * (2 * cycle_index[None, :] + 1) % (2 * cycle_count)
    angles = phase_index.astype(jnp.float32) * (math.pi / cycle_count)
    wave_float = wave_number.astype(jnp.float32)
    divisor = 4.0 * wave_float * wave_float - 1.0
    series = jnp.sum(jnp.cos(angles) / divisor[:, None], axis=0)
    return 2.0 / cycle_count * (1.0 - 2.0 * series)


def legendre_tables(orders, cycle_count, degree_count):
    cosine, log_sine = cycle_geometry(cycle_count)
    order_int = orders[:, None]
    order_float = orders.astype(jnp.float32)[:, None]
    counter = jnp.arange(1, degree_count, dtype=jnp.int32)
    counter_float = counter.astype(jnp.float32)
    factors = jnp.where(
        counter[None, :] <= order_int, jnp.log(1.0 - 0.5 / counter_float)[None, :], 0.0
    )
    log_start = (
        0.5 * jnp.log((2.0 * order_float + 1.0) / (4.0 * math.pi))
        + 0.5 * jnp.sum(factors, axis=1, keepdims=True)
        + order_float * log_sine[None, :]
    )
    even_first = order_int % 2 == 0

    def advance(carry_state, degree):
        previous, latest, log_scale = carry_state
        degree_float = degree.astype(jnp.float32)
        below_float = degree_float - 1.0
        coef_first = jnp.sqrt(
            jnp.maximum(4.0 * degree_float * degree_float - 1.0, 0.0)
            / jnp.maximum(degree_float * degree_float - order_float * order_float, 1.0)
        )
        coef_second = jnp.sqrt(
            jnp.maximum(below_float * below_float - order_float * order_float, 0.0)
            / jnp.maximum(4.0 * below_float * below_float - 1.0, 1.0)
        )
        current = coef_first * (cosine[None, :] * latest - coef_second * previous)
        current = jnp.where(
            degree == order_int + 1,
            jnp.sqrt(2.0 * order_float + 3.0) * cosine[None, :] * latest,
            current,
        )
        current = jnp.where(degree == order_int, 1.0, current)
        current = jnp.where(degree < order_int, 0.0, current)
        result = current * jnp.exp(log_scale)
        too_large = jnp.abs(current) > two_power
        factor = jnp.where(too_large, inverse_power, 1.0)
        next_state = (
            latest * factor,
            current * factor,
            log_scale + jnp.where(too_large, log_jump, 0.0),
        )
        return (next_state, result)

    def pair_step(carry_state, half_degree):
        carry_state, lower_row = advance(carry_state, 2 * half_degree)
        carry_state, upper_row = advance(carry_state, 2 * half_degree + 1)
        even_row = jnp.where(even_first, lower_row, upper_row).astype(jnp.bfloat16)
        odd_row = jnp.where(even_first, upper_row, lower_row).astype(jnp.bfloat16)
        return (carry_state, (even_row, odd_row))

    zero_rows = jnp.zeros((orders.shape[0], cycle_count // 2), jnp.float32)
    initial = (zero_rows, zero_rows, log_start)
    final_state, tables = lax.scan(
        pair_step, initial, jnp.arange(degree_count // 2, dtype=jnp.int32), unroll=32
    )
    return tables


def fourier_table(orders_all, point_count):
    longitudes = jnp.arange(point_count, dtype=jnp.int32)
    phase_index = orders_all[:, None] * longitudes[None, :] % point_count
    angles = phase_index.astype(jnp.float32) * (2.0 * math.pi / point_count)
    return jnp.stack([jnp.cos(angles), -jnp.sin(angles)], axis=1).astype(jnp.bfloat16)


def synthesize(spectra, tables, orders):
    even_first = (orders % 2 == 0)[None, None, :, None, None]
    paired = spectra.reshape(spectra.shape[:-1] + (spectra.shape[-1] // 2, 2))
    even_part = jnp.where(even_first, paired[..., 0], paired[..., 1])
    odd_part = jnp.where(even_first, paired[..., 1], paired[..., 0])
    symmetric = jnp.einsum(
        "csmri,imj->csmrj", even_part, tables[0], preferred_element_type=jnp.float32
    )
    antisymmetric = jnp.einsum(
        "csmri,imj->csmrj", odd_part, tables[1], preferred_element_type=jnp.float32
    )
    north_side = symmetric + antisymmetric
    south_side = symmetric - antisymmetric
    return jnp.concatenate([north_side, jnp.flip(south_side, axis=-1)], axis=-1).astype(
        jnp.bfloat16
    )


def analyze(gridded, tables, orders, weights):
    half_count = gridded.shape[-1] // 2
    north_side = gridded[..., :half_count].astype(jnp.float32)
    south_side = jnp.flip(gridded[..., half_count:], axis=-1).astype(jnp.float32)
    even_side = (weights * (north_side + south_side)).astype(jnp.bfloat16)
    odd_side = (weights * (north_side - south_side)).astype(jnp.bfloat16)
    even_part = jnp.einsum(
        "csmrj,imj->csmri", even_side, tables[0], preferred_element_type=jnp.float32
    )
    odd_part = jnp.einsum(
        "csmrj,imj->csmri", odd_side, tables[1], preferred_element_type=jnp.float32
    )
    even_first = (orders % 2 == 0)[None, None, :, None, None]
    low_side = jnp.where(even_first, even_part, odd_part)
    high_side = jnp.where(even_first, odd_part, even_part)
    stacked = jnp.stack([low_side, high_side], axis=-1)
    return stacked.reshape(stacked.shape[:-2] + (2 * stacked.shape[-2],))


def shards(strain_spec, order_map, viscosity, radial_weight):
    component_count, shell_count, order_count, complex_parts, degree_count = strain_spec.shape
    block_count = lax.axis_size("blk")
    cycle_local = viscosity.shape[1]
    cycle_count = cycle_local * block_count
    point_count = viscosity.shape[2]
    my_orders = lax.dynamic_slice_in_dim(
        order_map, lax.axis_index("blk") * order_count, order_count
    )
    tables = legendre_tables(my_orders, cycle_count, degree_count)
    weights = fejer_weights(cycle_count)
    wave_table = fourier_table(order_map, point_count).reshape(
        block_count, order_count, 2, point_count
    )
    doubling = (
        jnp.where(order_map == 0, 1.0, 2.0).astype(jnp.bfloat16).reshape(block_count, order_count)
    )
    norm_factor = 2.0 * math.pi / point_count
    gridded = synthesize(strain_spec, tables, my_orders)
    item_count = gridded.shape[0]
    pieces = gridded.reshape(item_count, shell_count, order_count, 2, block_count, cycle_local)
    outgoing = pieces.transpose(0, 1, 4, 2, 3, 5).reshape(
        item_count, shell_count, block_count, order_count * 2 * cycle_local
    )
    returns = []
    for component in range(component_count):
        received = lax.all_to_all(
            outgoing[component : component + 1], "blk", split_axis=2, concat_axis=2, tiled=True
        )
        cycle_item_count = received.shape[0]
        blocks = received.reshape(
            cycle_item_count, shell_count, block_count, order_count, 2, cycle_local
        )
        blocks = blocks * doubling[None, None, :, :, None, None]
        grid_field = jnp.einsum(
            "csdxrj,dxrk->csjk", blocks, wave_table, preferred_element_type=jnp.float32
        )
        stress = (viscosity[None] * grid_field).astype(jnp.bfloat16)
        spectra = jnp.einsum(
            "csjk,dxrk->csdxrj", stress, wave_table, preferred_element_type=jnp.float32
        )
        spectra = (spectra * norm_factor).astype(jnp.bfloat16)
        returns.append(
            lax.all_to_all(
                spectra.reshape(
                    cycle_item_count, shell_count, block_count, order_count * 2 * cycle_local
                ),
                "blk",
                split_axis=2,
                concat_axis=2,
                tiled=True,
            )
        )
    returned = jnp.concatenate(returns, axis=0)
    item_count = returned.shape[0]
    pieces = returned.reshape(item_count, shell_count, block_count, order_count, 2, cycle_local)
    coefficient = analyze(
        pieces.transpose(0, 1, 3, 4, 2, 5).reshape(
            item_count, shell_count, order_count, 2, cycle_count
        ),
        tables,
        my_orders,
        weights,
    )
    stress_spec = coefficient.astype(jnp.bfloat16)
    weighted = jnp.sum(coefficient * radial_weight[None, :, None, None, None], axis=1)
    summed = lax.psum(weighted.astype(jnp.bfloat16), "shell").astype(jnp.float32)
    share_size = degree_count // lax.axis_size("shell")
    integrated = lax.dynamic_slice_in_dim(
        summed, lax.axis_index("shell") * share_size, share_size, 3
    )
    return (stress_spec, integrated)


def solution(mesh):
    return jax.shard_map(
        shards,
        mesh=mesh,
        in_specs=(P(None, "shell", "blk", None, None), P(), P("shell", "blk", None), P("shell")),
        out_specs=(P(None, "shell", "blk", None, None), P(None, "blk", None, "shell")),
        check_vma=False,
    )
```

profile of v0, /device:TPU:1, one launch (start us, length us, event | category | flops | bytes accessed | tf_op | source)
XLA Modules:
  0.0 964.2 jit_solution(11079613722453055264)
XLA Ops:
  8.4 453.0 %while.23 = (s32[]{:T(128)}, f32[16,512]{1,0:T(8,128)S(1)}, f32[16,512]{1,0:T(8,128)S(1)}, f32[16,512]{1,0:T(8,128)S(1)}, bf16[16,32,16,512]{3,2,1,0:T(8,128)(2,...) while((s32[]{:T(128)}, f32[16,512]{1,0:T(8,128)S(1)}, ...), condition=%wide.region_2.3_spmd.clone.clone, body=%wide.region_1.2_spmd.clone.clone.sunk | while | flops 11857313 | bytes 9983139 | solution.py:85
  482.1 12.5 %fusion.457 = f32[16,512,6,2]{1,2,3,0:T(8,128)S(1)} fusion(bf16[512,16,512,1]{2,1,0,3:T(8,128)(2,1)} %bitcast.1497, bf16[6,16,2,512]{3,1,2,0:T(8,128)(2,1)S(1)} %get-tuple-element.1382), kind=kOutput, calls=%fused_computation.1301 | convolution fusion | flops 100663296 | bytes 8978432 | tf_op jit(solution)/shard_map/csmri,imj->csmrj/dot_general | solution.py:106
  494.6 9.2 fusion.459
  511.9 12.9 %all-to-all-start = ((bf16[64,2,256]{2,1,0:T(2,128)(2,1)}), bf16[64,2,256]{2,1,0:T(2,128)(2,1)S(1)}, u32[]{:S(2)}, u32[]{:S(2)}) async-start(bf16[64,2,256]{2,1,0:T(2,128)(2,1)} %reshape.4644), calls=%async_computation | async-start | bytes 131072 | tf_op jit(solution)/shard_map/all_to_all | solution.py:161
  538.3 37.1 %cosine_convert_fusion = (bf16[64,16,1,2048]{3,0,1,2:T(8,128)(2,1)}, bf16[64,16,1,2048]{3,0,1,2:T(8,128)(2,1)}) fusion(s32[64,16]{0,1:T(8,128)S(1)} %copy.241), kind=kLoop, calls=%fused_computation.1295 | loop fusion | flops 35651584 | bytes 8392704 | tf_op jit(solution)/shard_map/convert.6
  577.2 10.2 %all-to-all-start.4 = ((bf16[64,2,256]{2,1,0:T(2,128)(2,1)}), bf16[64,2,256]{2,1,0:T(2,128)(2,1)S(1)}, u32[]{:S(2)}, u32[]{:S(2)}) async-start(bf16[64,2,256]{2,1,0:T(2,128)(2,1)} %reshape.4652), calls=%async_computation.4 | async-start | bytes 131072 | tf_op jit(solution)/shard_map/all_to_all | solution.py:161
  587.4 7.6 pad_maximum_fusion
  596.9 10.2 %all-to-all-start.6 = ((bf16[64,2,256]{2,1,0:T(2,128)(2,1)}), bf16[64,2,256]{2,1,0:T(2,128)(2,1)S(1)}, u32[]{:S(2)}, u32[]{:S(2)}) async-start(bf16[64,2,256]{2,1,0:T(2,128)(2,1)} %reshape.4656), calls=%async_computation.6 | async-start | bytes 131072 | tf_op jit(solution)/shard_map/all_to_all | solution.py:161
  630.0 7.4 all-to-all-start.10
  646.9 8.3 fusion.526
  661.7 8.3 fusion.520
  671.9 10.2 %all-to-all-start.9 = ((bf16[64,2,256]{2,1,0:T(2,128)(2,1)}), bf16[64,2,256]{2,1,0:T(2,128)(2,1)S(1)}, u32[]{:S(2)}, u32[]{:S(2)}) async-start(bf16[64,2,256]{2,1,0:T(2,128)(2,1)} %reshape.4662), calls=%async_computation.9 | async-start | bytes 131072 | tf_op jit(solution)/shard_map/all_to_all | solution.py:178
  682.1 8.3 fusion.514
  692.3 10.4 %all-to-all-start.7 = ((bf16[64,2,256]{2,1,0:T(2,128)(2,1)}), bf16[64,2,256]{2,1,0:T(2,128)(2,1)S(1)}, u32[]{:S(2)}, u32[]{:S(2)}) async-start(bf16[64,2,256]{2,1,0:T(2,128)(2,1)} %reshape.4658), calls=%async_computation.7 | async-start | bytes 131072 | tf_op jit(solution)/shard_map/all_to_all | solution.py:178
  702.7 8.3 fusion.508
  712.8 10.3 %all-to-all-start.5 = ((bf16[64,2,256]{2,1,0:T(2,128)(2,1)}), bf16[64,2,256]{2,1,0:T(2,128)(2,1)S(1)}, u32[]{:S(2)}, u32[]{:S(2)}) async-start(bf16[64,2,256]{2,1,0:T(2,128)(2,1)} %reshape.4654), calls=%async_computation.5 | async-start | bytes 131072 | tf_op jit(solution)/shard_map/all_to_all | solution.py:178
  723.1 8.3 fusion.502
  733.3 10.2 %all-to-all-start.3 = ((bf16[64,2,256]{2,1,0:T(2,128)(2,1)}), bf16[64,2,256]{2,1,0:T(2,128)(2,1)S(1)}, u32[]{:S(2)}, u32[]{:S(2)}) async-start(bf16[64,2,256]{2,1,0:T(2,128)(2,1)} %reshape.4650), calls=%async_computation.3 | async-start | bytes 131072 | tf_op jit(solution)/shard_map/all_to_all | solution.py:178
  743.5 8.3 fusion.496
  753.7 10.2 %all-to-all-start.1 = ((bf16[64,2,256]{2,1,0:T(2,128)(2,1)}), bf16[64,2,256]{2,1,0:T(2,128)(2,1)S(1)}, u32[]{:S(2)}, u32[]{:S(2)}) async-start(bf16[64,2,256]{2,1,0:T(2,128)(2,1)} %reshape.4646), calls=%async_computation.1 | async-start | bytes 131072 | tf_op jit(solution)/shard_map/all_to_all | solution.py:178
  765.0 8.0 all-to-all-done.1
  783.6 12.4 %fusion.461 = f32[16,512,6,2]{1,2,3,0:T(8,128)S(1)} fusion(bf16[512,16,512,1]{2,1,0,3:T(8,128)(2,1)} %bitcast.1493, bf16[6,16,2,512]{3,1,2,0:T(8,128)(2,1)S(1)} %get-tuple-element.1379), kind=kOutput, calls=%fused_computation.1305 | convolution fusion | flops 100663296 | bytes 8978432 | tf_op jit(solution)/shard_map/csmrj,imj->csmri/dot_general | solution.py:122
  796.0 12.5 %fusion.455 = f32[16,512,6,2]{1,2,3,0:T(8,128)S(1)} fusion(bf16[512,16,512,1]{2,1,0,3:T(8,128)(2,1)} %bitcast.1498, bf16[6,16,2,512]{3,1,2,0:T(8,128)(2,1)S(1)} %get-tuple-element.1380), kind=kOutput, calls=%fused_computation.1299 | convolution fusion | flops 100663296 | bytes 8978432 | tf_op jit(solution)/shard_map/csmrj,imj->csmri/dot_general | solution.py:125
  818.9 135.9 %all-reduce.2.cloned.1.call-done = bf16[6,16,2,1024]{1,3,2,0:T(8,128)(2,1)} async-done(((bf16[6,16,2,1024]{1,3,2,0:T(8,128)(2,1)}), bf16[6,16,2,1024]{1,3,2,0:T(8,128)(2,1)}) %all-reduce.2.cloned.1.call-update) | async-done | bytes 393232 | tf_op jit(solution)/shard_map/psum | solution.py:201
  (1090 shorter events, 232.8 us)
Async XLA Ops:
  8.4 453.0 %copy-start.2 = (bf16[6,1,16,2,1024]{4,3,2,1,0:T(2,128)(2,1)S(1)}, bf16[6,1,16,2,1024]{4,3,2,1,0:T(2,128)(2,1)}, u32[]{:S(2)}) copy-start(bf16[6,1,16,2,1024]{4,3,2,1,0:T(2,128)(2,1)} %param.6) | copy-start | bytes 1179652
  482.0 12.6 %slice-start = ((s8[8388608]{0:T(1024)(128)(4,1)}), s8[4194304]{0:T(1024)(128)(4,1)S(1)}, s32[]{:S(2)}) async-start(s8[8388608]{0:T(1024)(128)(4,1)} %bitcast.1494), calls=%async_computation.13 | async-start | bytes 8388608
  482.1 12.5 %slice-start.1 = ((s8[8388608]{0:T(1024)(128)(4,1)}), s8[4194304]{0:T(1024)(128)(4,1)S(1)}, s32[]{:S(2)}) async-start(s8[8388608]{0:T(1024)(128)(4,1)} %bitcast.1494), calls=%async_computation.14 | async-start | bytes 8388608
  503.8 21.0 %copy-start.3 = (s32[1024]{0:T(1024)S(1)}, s32[1024]{0:T(1024)}, u32[]{:S(2)}) copy-start(s32[1024]{0:T(1024)} %param.7) | copy-start | bytes 12292
  511.9 21.8 %all-to-all-start = ((bf16[64,2,256]{2,1,0:T(2,128)(2,1)}), bf16[64,2,256]{2,1,0:T(2,128)(2,1)S(1)}, u32[]{:S(2)}, u32[]{:S(2)}) async-start(bf16[64,2,256]{2,1,0:T(2,128)(2,1)} %reshape.4644), calls=%async_computation | async-start | bytes 131072 | tf_op jit(solution)/shard_map/all_to_all | solution.py:161
  533.7 43.6 %all-to-all-start.2 = ((bf16[64,2,256]{2,1,0:T(2,128)(2,1)}), bf16[64,2,256]{2,1,0:T(2,128)(2,1)S(1)}, u32[]{:S(2)}, u32[]{:S(2)}) async-start(bf16[64,2,256]{2,1,0:T(2,128)(2,1)} %reshape.4648), calls=%async_computation.2 | async-start | bytes 131072 | tf_op jit(solution)/shard_map/all_to_all | solution.py:161
  577.2 19.6 %all-to-all-start.4 = ((bf16[64,2,256]{2,1,0:T(2,128)(2,1)}), bf16[64,2,256]{2,1,0:T(2,128)(2,1)S(1)}, u32[]{:S(2)}, u32[]{:S(2)}) async-start(bf16[64,2,256]{2,1,0:T(2,128)(2,1)} %reshape.4652), calls=%async_computation.4 | async-start | bytes 131072 | tf_op jit(solution)/shard_map/all_to_all | solution.py:161
  587.4 59.5 %copy-start = (f32[1,16,2048]{2,1,0:T(8,128)S(1)}, f32[1,16,2048]{2,1,0:T(8,128)}, u32[]{:S(2)}) copy-start(f32[1,16,2048]{2,1,0:T(8,128)} %param.8) | copy-start | bytes 393220
  596.9 19.4 %all-to-all-start.6 = ((bf16[64,2,256]{2,1,0:T(2,128)(2,1)}), bf16[64,2,256]{2,1,0:T(2,128)(2,1)S(1)}, u32[]{:S(2)}, u32[]{:S(2)}) async-start(bf16[64,2,256]{2,1,0:T(2,128)(2,1)} %reshape.4656), calls=%async_computation.6 | async-start | bytes 131072 | tf_op jit(solution)/shard_map/all_to_all | solution.py:161
  616.2 13.8 %all-to-all-start.8 = ((bf16[64,2,256]{2,1,0:T(2,128)(2,1)}), bf16[64,2,256]{2,1,0:T(2,128)(2,1)S(1)}, u32[]{:S(2)}, u32[]{:S(2)}) async-start(bf16[64,2,256]{2,1,0:T(2,128)(2,1)} %reshape.4660), calls=%async_computation.8 | async-start | bytes 131072 | tf_op jit(solution)/shard_map/all_to_all | solution.py:161
  630.0 16.6 %all-to-all-start.10 = ((bf16[64,2,256]{2,1,0:T(2,128)(2,1)}), bf16[64,2,256]{2,1,0:T(2,128)(2,1)S(1)}, u32[]{:S(2)}, u32[]{:S(2)}) async-start(bf16[64,2,256]{2,1,0:T(2,128)(2,1)} %reshape.4664), calls=%async_computation.10 | async-start | bytes 131072 | tf_op jit(solution)/shard_map/all_to_all | solution.py:161
  657.1 14.8 %all-to-all-start.11 = ((bf16[64,2,256]{2,1,0:T(2,128)(2,1)}), bf16[64,2,256]{2,1,0:T(2,128)(2,1)S(1)}, u32[]{:S(2)}, u32[]{:S(2)}) async-start(bf16[64,2,256]{2,1,0:T(2,128)(2,1)} %reshape.4666), calls=%async_computation.11 | async-start | bytes 131072 | tf_op jit(solution)/shard_map/all_to_all | solution.py:178
  671.9 20.4 %all-to-all-start.9 = ((bf16[64,2,256]{2,1,0:T(2,128)(2,1)}), bf16[64,2,256]{2,1,0:T(2,128)(2,1)S(1)}, u32[]{:S(2)}, u32[]{:S(2)}) async-start(bf16[64,2,256]{2,1,0:T(2,128)(2,1)} %reshape.4662), calls=%async_computation.9 | async-start | bytes 131072 | tf_op jit(solution)/shard_map/all_to_all | solution.py:178
  692.3 20.6 %all-to-all-start.7 = ((bf16[64,2,256]{2,1,0:T(2,128)(2,1)}), bf16[64,2,256]{2,1,0:T(2,128)(2,1)S(1)}, u32[]{:S(2)}, u32[]{:S(2)}) async-start(bf16[64,2,256]{2,1,0:T(2,128)(2,1)} %reshape.4658), calls=%async_computation.7 | async-start | bytes 131072 | tf_op jit(solution)/shard_map/all_to_all | solution.py:178
  712.8 20.5 %all-to-all-start.5 = ((bf16[64,2,256]{2,1,0:T(2,128)(2,1)}), bf16[64,2,256]{2,1,0:T(2,128)(2,1)S(1)}, u32[]{:S(2)}, u32[]{:S(2)}) async-start(bf16[64,2,256]{2,1,0:T(2,128)(2,1)} %reshape.4654), calls=%async_computation.5 | async-start | bytes 131072 | tf_op jit(solution)/shard_map/all_to_all | solution.py:178
  733.3 20.4 %all-to-all-start.3 = ((bf16[64,2,256]{2,1,0:T(2,128)(2,1)}), bf16[64,2,256]{2,1,0:T(2,128)(2,1)S(1)}, u32[]{:S(2)}, u32[]{:S(2)}) async-start(bf16[64,2,256]{2,1,0:T(2,128)(2,1)} %reshape.4650), calls=%async_computation.3 | async-start | bytes 131072 | tf_op jit(solution)/shard_map/all_to_all | solution.py:178
  753.7 19.4 %all-to-all-start.1 = ((bf16[64,2,256]{2,1,0:T(2,128)(2,1)}), bf16[64,2,256]{2,1,0:T(2,128)(2,1)S(1)}, u32[]{:S(2)}, u32[]{:S(2)}) async-start(bf16[64,2,256]{2,1,0:T(2,128)(2,1)} %reshape.4646), calls=%async_computation.1 | async-start | bytes 131072 | tf_op jit(solution)/shard_map/all_to_all | solution.py:178
  763.9 190.9 %all-reduce.2.cloned.1.call-start = ((), (), s32[]{:S(2)}) async-start(), calls=%async_computation.12 | async-start | bytes 6291456 | tf_op jit(solution)/shard_map/psum | solution.py:201
  773.4 0.9 copy-start.1
Sparse Core Ops, SparseCore 0:
  814.6 140.1 all-reduce.1
where the time goes:
time: 975 us; the launch traced here: 964 us
  loops' own time  339 us (35%)
  waiting for transfers between devices  168 us (17%)
  other arithmetic  139 us (14%)
  starting transfers between devices  106 us (11%)
  local copies, waits for them, and re-layouts  100 us (10%)
  matrix products  96.4 us (10%)
  between operations  15.6 us (2%)
    another operation x1, loops' own time, legendre_tables(): lax.scan(pair_step, initial, jnp.arange(degree_count // 2, dtype=jnp.int3...  339 us
    psum x1, waiting for transfers between devices, shards(): lax.psum(weighted.astype(jnp.bfloat16), 'shell').astype(jnp.float32)  136 us
    while x496, other arithmetic  56.9 us
    all_to_all x6, starting transfers between devices, shards(): lax.all_to_all(spectra.reshape(cycle_item_count, shell_count, block_count...  55.8 us
    all_to_all x6, starting transfers between devices, shards(): lax.all_to_all(outgoing[component:component + 1], 'blk', split_axis=2, co...  50 us
    dot_general x6, matrix products, shards(): jnp.einsum('csjk,dxrk->csdxrj', stress, wave_table, preferred_element_typ...  49.8 us
    another operation x4, other arithmetic  37.2 us
    all_to_all x6, waiting for transfers between devices, shards(): lax.all_to_all(outgoing[component:component + 1], 'blk', split_axis=2, co...  24.3 us
  transfers between devices with their start and end apart: 13, of which 6 were waited for; matrix products, arithmetic and copies ran while one was open for 12% of the time, Pallas kernels for 0%

commit v1 on v0

--- a/solution.py
+++ b/solution.py
@@ -198,7 +198,11 @@
     )
     stress_spec = coefficient.astype(jnp.bfloat16)
     weighted = jnp.sum(coefficient * radial_weight[None, :, None, None, None], axis=1)
-    summed = lax.psum(weighted.astype(jnp.bfloat16), "shell").astype(jnp.float32)
+
+    def open_the_sheets(my_tile, comm_axis):
+        return lax.all_gather(my_tile, comm_axis).sum(axis=0)
+
+    summed = open_the_sheets(weighted.astype(jnp.bfloat16), "shell").astype(jnp.float32)
     share_size = degree_count // lax.axis_size("shell")
     integrated = lax.dynamic_slice_in_dim(
         summed, lax.axis_index("shell") * share_size, share_size, 3

time: 975 us -> 882 us (0.905)
  waiting for transfers between devices: 168 us -> 66.5 us
    psum x1 -> x0, waiting for transfers between devices: 136 us -> none  [shards(): lax.psum(weighted.astype(jnp.bfloat16), 'shell').astype(jnp.float32)]
    all_gather x0 -> x1, waiting for transfers between devices: none -> 33.7 us  [open_the_sheets(): return lax.all_gather(my_tile, comm_axis).sum(axis=0)]
  transfers between devices with their start and end apart: 13 -> 13, of which waited for: 6 -> 6; matrix products, arithmetic and copies ran while one was open for 12% -> 14% of each run, Pallas kernels for 0% -> 0%
where the time goes in v1:
time: 882 us; the launch traced here: 871 us
  loops' own time  339 us (38%)
  other arithmetic  140 us (16%)
  local copies, waits for them, and re-layouts  107 us (12%)
  starting transfers between devices  106 us (12%)
  matrix products  96.4 us (11%)
  waiting for transfers between devices  66.5 us (8%)
  between operations  15.6 us (2%)
    another operation x1, loops' own time, legendre_tables(): lax.scan(pair_step, initial, jnp.arange(degree_count // 2, dtype=jnp.int3...  339 us
    while x496, other arithmetic  56.9 us
    all_to_all x6, starting transfers between devices, shards(): lax.all_to_all(spectra.reshape(cycle_item_count, shell_count, block_count...  55.8 us
    all_to_all x6, starting transfers between devices, shards(): lax.all_to_all(outgoing[component:component + 1], 'blk', split_axis=2, co...  49.8 us
    dot_general x6, matrix products, shards(): jnp.einsum('csjk,dxrk->csdxrj', stress, wave_table, preferred_element_typ...  49.8 us
    another operation x4, other arithmetic  37.2 us
    all_gather x1, waiting for transfers between devices, open_the_sheets(): return lax.all_gather(my_tile, comm_axis).sum(axis=0)  33.7 us
    all_to_all x6, waiting for transfers between devices, shards(): lax.all_to_all(outgoing[component:component + 1], 'blk', split_axis=2, co...  24.7 us
  transfers between devices with their start and end apart: 13, of which 6 were waited for; matrix products, arithmetic and copies ran while one was open for 14% of the time, Pallas kernels for 0%

profile of v1, /device:TPU:1, one launch (start us, length us, event | category | flops | bytes accessed | tf_op | source)
XLA Modules:
  0.0 870.8 jit_solution(1037555196054859497)
XLA Ops:
  8.4 453.0 %while.23 = (s32[]{:T(128)}, f32[16,512]{1,0:T(8,128)S(1)}, f32[16,512]{1,0:T(8,128)S(1)}, f32[16,512]{1,0:T(8,128)S(1)}, bf16[16,32,16,512]{3,2,1,0:T(8,128)(2,...) while((s32[]{:T(128)}, f32[16,512]{1,0:T(8,128)S(1)}, ...), condition=%wide.region_2.3_spmd.clone.clone, body=%wide.region_1.2_spmd.clone.clone.sunk | while | flops 11857313 | bytes 9983139 | solution.py:85
  482.2 12.5 %fusion.457 = f32[16,512,6,2]{1,2,3,0:T(8,128)S(1)} fusion(bf16[512,16,512,1]{2,1,0,3:T(8,128)(2,1)} %bitcast.1497, bf16[6,16,2,512]{3,1,2,0:T(8,128)(2,1)S(1)} %get-tuple-element.1382), kind=kOutput, calls=%fused_computation.1301 | convolution fusion | flops 100663296 | bytes 8978432 | tf_op jit(solution)/shard_map/csmri,imj->csmrj/dot_general | solution.py:106
  494.7 9.2 %fusion.459 = f32[16,512,6,2]{1,2,3,0:T(8,128)S(1)} fusion(bf16[512,16,512,1]{2,1,0,3:T(8,128)(2,1)S(1)} %bitcast.1496, bf16[6,16,2,512]{3,1,2,0:T(8,128)(2,1)S(1)} %get-tuple-element.1381), kind=kOutput, calls=%fused_computation.1303 | convolution fusion | flops 100663296 | bytes 8978432 | tf_op jit(solution)/shard_map/csmri,imj->csmrj/dot_general | solution.py:103
  511.7 12.9 %all-to-all-start = ((bf16[64,2,256]{2,1,0:T(2,128)(2,1)}), bf16[64,2,256]{2,1,0:T(2,128)(2,1)S(1)}, u32[]{:S(2)}, u32[]{:S(2)}) async-start(bf16[64,2,256]{2,1,0:T(2,128)(2,1)} %reshape.4657), calls=%async_computation | async-start | bytes 131072 | tf_op jit(solution)/shard_map/all_to_all | solution.py:161
  538.2 37.1 %cosine_convert_fusion = (bf16[64,16,1,2048]{3,0,1,2:T(8,128)(2,1)}, bf16[64,16,1,2048]{3,0,1,2:T(8,128)(2,1)}) fusion(s32[64,16]{0,1:T(8,128)S(1)} %copy.242), kind=kLoop, calls=%fused_computation.1295 | loop fusion | flops 35651584 | bytes 8392704 | tf_op jit(solution)/shard_map/convert.7
  577.0 10.2 %all-to-all-start.4 = ((bf16[64,2,256]{2,1,0:T(2,128)(2,1)}), bf16[64,2,256]{2,1,0:T(2,128)(2,1)S(1)}, u32[]{:S(2)}, u32[]{:S(2)}) async-start(bf16[64,2,256]{2,1,0:T(2,128)(2,1)} %reshape.4665), calls=%async_computation.4 | async-start | bytes 131072 | tf_op jit(solution)/shard_map/all_to_all | solution.py:161
  587.2 7.6 pad_maximum_fusion
  596.5 10.2 %all-to-all-start.6 = ((bf16[64,2,256]{2,1,0:T(2,128)(2,1)}), bf16[64,2,256]{2,1,0:T(2,128)(2,1)S(1)}, u32[]{:S(2)}, u32[]{:S(2)}) async-start(bf16[64,2,256]{2,1,0:T(2,128)(2,1)} %reshape.4669), calls=%async_computation.6 | async-start | bytes 131072 | tf_op jit(solution)/shard_map/all_to_all | solution.py:161
  608.4 7.4 all-to-all-done.6
  646.4 8.3 fusion.526
  661.1 8.3 fusion.520
  671.2 10.2 %all-to-all-start.9 = ((bf16[64,2,256]{2,1,0:T(2,128)(2,1)}), bf16[64,2,256]{2,1,0:T(2,128)(2,1)S(1)}, u32[]{:S(2)}, u32[]{:S(2)}) async-start(bf16[64,2,256]{2,1,0:T(2,128)(2,1)} %reshape.4675), calls=%async_computation.9 | async-start | bytes 131072 | tf_op jit(solution)/shard_map/all_to_all | solution.py:178
  681.4 8.3 fusion.514
  691.4 10.4 %all-to-all-start.7 = ((bf16[64,2,256]{2,1,0:T(2,128)(2,1)}), bf16[64,2,256]{2,1,0:T(2,128)(2,1)S(1)}, u32[]{:S(2)}, u32[]{:S(2)}) async-start(bf16[64,2,256]{2,1,0:T(2,128)(2,1)} %reshape.4671), calls=%async_computation.7 | async-start | bytes 131072 | tf_op jit(solution)/shard_map/all_to_all | solution.py:178
  701.8 8.3 fusion.508
  711.8 10.3 %all-to-all-start.5 = ((bf16[64,2,256]{2,1,0:T(2,128)(2,1)}), bf16[64,2,256]{2,1,0:T(2,128)(2,1)S(1)}, u32[]{:S(2)}, u32[]{:S(2)}) async-start(bf16[64,2,256]{2,1,0:T(2,128)(2,1)} %reshape.4667), calls=%async_computation.5 | async-start | bytes 131072 | tf_op jit(solution)/shard_map/all_to_all | solution.py:178
  722.1 8.3 fusion.502
  732.2 10.2 %all-to-all-start.3 = ((bf16[64,2,256]{2,1,0:T(2,128)(2,1)}), bf16[64,2,256]{2,1,0:T(2,128)(2,1)S(1)}, u32[]{:S(2)}, u32[]{:S(2)}) async-start(bf16[64,2,256]{2,1,0:T(2,128)(2,1)} %reshape.4663), calls=%async_computation.3 | async-start | bytes 131072 | tf_op jit(solution)/shard_map/all_to_all | solution.py:178
  742.4 8.3 fusion.496
  752.4 10.2 %all-to-all-start.1 = ((bf16[64,2,256]{2,1,0:T(2,128)(2,1)}), bf16[64,2,256]{2,1,0:T(2,128)(2,1)S(1)}, u32[]{:S(2)}, u32[]{:S(2)}) async-start(bf16[64,2,256]{2,1,0:T(2,128)(2,1)} %reshape.4659), calls=%async_computation.1 | async-start | bytes 131072 | tf_op jit(solution)/shard_map/all_to_all | solution.py:178
  763.8 8.0 all-to-all-done.1
  782.3 12.4 %fusion.461 = f32[16,512,6,2]{1,2,3,0:T(8,128)S(1)} fusion(bf16[512,16,512,1]{2,1,0,3:T(8,128)(2,1)} %bitcast.1493, bf16[6,16,2,512]{3,1,2,0:T(8,128)(2,1)S(1)} %get-tuple-element.1379), kind=kOutput, calls=%fused_computation.1305 | convolution fusion | flops 100663296 | bytes 8978432 | tf_op jit(solution)/shard_map/csmrj,imj->csmri/dot_general | solution.py:122
  794.7 12.5 %fusion.455 = f32[16,512,6,2]{1,2,3,0:T(8,128)S(1)} fusion(bf16[512,16,512,1]{2,1,0,3:T(8,128)(2,1)} %bitcast.1498, bf16[6,16,2,512]{3,1,2,0:T(8,128)(2,1)S(1)} %get-tuple-element.1380), kind=kOutput, calls=%fused_computation.1299 | convolution fusion | flops 100663296 | bytes 8978432 | tf_op jit(solution)/shard_map/csmrj,imj->csmri/dot_general | solution.py:125
  826.9 33.7 %all-gather.2.cloned.1.call-done = bf16[4,6,16,2,1024]{4,2,3,1,0:T(8,128)(2,1)} async-done(((bf16[1,6,16,2,1024]{4,2,3,1,0:T(8,128)(2,1)}), bf16[4,6,16,2,1024]{4,2,3,1,0:T(8,128)(2,1)}) %all-gather.2.cloned.1.call-update) | async-done | bytes 1572880 | tf_op jit(solution)/shard_map/all_gather | solution.py:203
  (1095 shorter events, 241.3 us)
Async XLA Ops:
  8.4 453.1 %copy-start.3 = (bf16[6,1,16,2,1024]{4,3,2,1,0:T(2,128)(2,1)S(1)}, bf16[6,1,16,2,1024]{4,3,2,1,0:T(2,128)(2,1)}, u32[]{:S(2)}) copy-start(bf16[6,1,16,2,1024]{4,3,2,1,0:T(2,128)(2,1)} %param.6) | copy-start | bytes 1179652
  482.1 12.6 %slice-start = ((s8[8388608]{0:T(1024)(128)(4,1)}), s8[4194304]{0:T(1024)(128)(4,1)S(1)}, s32[]{:S(2)}) async-start(s8[8388608]{0:T(1024)(128)(4,1)} %bitcast.1494), calls=%async_computation.13 | async-start | bytes 8388608
  482.2 12.5 %slice-start.1 = ((s8[8388608]{0:T(1024)(128)(4,1)}), s8[4194304]{0:T(1024)(128)(4,1)S(1)}, s32[]{:S(2)}) async-start(s8[8388608]{0:T(1024)(128)(4,1)} %bitcast.1494), calls=%async_computation.14 | async-start | bytes 8388608
  503.9 20.8 %copy-start.4 = (s32[1024]{0:T(1024)S(1)}, s32[1024]{0:T(1024)}, u32[]{:S(2)}) copy-start(s32[1024]{0:T(1024)} %param.7) | copy-start | bytes 12292
  511.7 21.8 %all-to-all-start = ((bf16[64,2,256]{2,1,0:T(2,128)(2,1)}), bf16[64,2,256]{2,1,0:T(2,128)(2,1)S(1)}, u32[]{:S(2)}, u32[]{:S(2)}) async-start(bf16[64,2,256]{2,1,0:T(2,128)(2,1)} %reshape.4657), calls=%async_computation | async-start | bytes 131072 | tf_op jit(solution)/shard_map/all_to_all | solution.py:161
  533.5 43.5 %all-to-all-start.2 = ((bf16[64,2,256]{2,1,0:T(2,128)(2,1)}), bf16[64,2,256]{2,1,0:T(2,128)(2,1)S(1)}, u32[]{:S(2)}, u32[]{:S(2)}) async-start(bf16[64,2,256]{2,1,0:T(2,128)(2,1)} %reshape.4661), calls=%async_computation.2 | async-start | bytes 131072 | tf_op jit(solution)/shard_map/all_to_all | solution.py:161
  577.0 19.5 %all-to-all-start.4 = ((bf16[64,2,256]{2,1,0:T(2,128)(2,1)}), bf16[64,2,256]{2,1,0:T(2,128)(2,1)S(1)}, u32[]{:S(2)}, u32[]{:S(2)}) async-start(bf16[64,2,256]{2,1,0:T(2,128)(2,1)} %reshape.4665), calls=%async_computation.4 | async-start | bytes 131072 | tf_op jit(solution)/shard_map/all_to_all | solution.py:161
  587.2 59.2 %copy-start = (f32[1,16,2048]{2,1,0:T(8,128)S(1)}, f32[1,16,2048]{2,1,0:T(8,128)}, u32[]{:S(2)}) copy-start(f32[1,16,2048]{2,1,0:T(8,128)} %param.8) | copy-start | bytes 393220
  596.5 19.4 %all-to-all-start.6 = ((bf16[64,2,256]{2,1,0:T(2,128)(2,1)}), bf16[64,2,256]{2,1,0:T(2,128)(2,1)S(1)}, u32[]{:S(2)}, u32[]{:S(2)}) async-start(bf16[64,2,256]{2,1,0:T(2,128)(2,1)} %reshape.4669), calls=%async_computation.6 | async-start | bytes 131072 | tf_op jit(solution)/shard_map/all_to_all | solution.py:161
  615.9 13.8 %all-to-all-start.8 = ((bf16[64,2,256]{2,1,0:T(2,128)(2,1)}), bf16[64,2,256]{2,1,0:T(2,128)(2,1)S(1)}, u32[]{:S(2)}, u32[]{:S(2)}) async-start(bf16[64,2,256]{2,1,0:T(2,128)(2,1)} %reshape.4673), calls=%async_computation.8 | async-start | bytes 131072 | tf_op jit(solution)/shard_map/all_to_all | solution.py:161
  629.7 16.5 %all-to-all-start.10 = ((bf16[64,2,256]{2,1,0:T(2,128)(2,1)}), bf16[64,2,256]{2,1,0:T(2,128)(2,1)S(1)}, u32[]{:S(2)}, u32[]{:S(2)}) async-start(bf16[64,2,256]{2,1,0:T(2,128)(2,1)} %reshape.4677), calls=%async_computation.10 | async-start | bytes 131072 | tf_op jit(solution)/shard_map/all_to_all | solution.py:161
  656.5 14.7 %all-to-all-start.11 = ((bf16[64,2,256]{2,1,0:T(2,128)(2,1)}), bf16[64,2,256]{2,1,0:T(2,128)(2,1)S(1)}, u32[]{:S(2)}, u32[]{:S(2)}) async-start(bf16[64,2,256]{2,1,0:T(2,128)(2,1)} %reshape.4679), calls=%async_computation.11 | async-start | bytes 131072 | tf_op jit(solution)/shard_map/all_to_all | solution.py:178
  671.2 20.2 %all-to-all-start.9 = ((bf16[64,2,256]{2,1,0:T(2,128)(2,1)}), bf16[64,2,256]{2,1,0:T(2,128)(2,1)S(1)}, u32[]{:S(2)}, u32[]{:S(2)}) async-start(bf16[64,2,256]{2,1,0:T(2,128)(2,1)} %reshape.4675), calls=%async_computation.9 | async-start | bytes 131072 | tf_op jit(solution)/shard_map/all_to_all | solution.py:178
  691.4 20.4 %all-to-all-start.7 = ((bf16[64,2,256]{2,1,0:T(2,128)(2,1)}), bf16[64,2,256]{2,1,0:T(2,128)(2,1)S(1)}, u32[]{:S(2)}, u32[]{:S(2)}) async-start(bf16[64,2,256]{2,1,0:T(2,128)(2,1)} %reshape.4671), calls=%async_computation.7 | async-start | bytes 131072 | tf_op jit(solution)/shard_map/all_to_all | solution.py:178
  711.8 20.3 %all-to-all-start.5 = ((bf16[64,2,256]{2,1,0:T(2,128)(2,1)}), bf16[64,2,256]{2,1,0:T(2,128)(2,1)S(1)}, u32[]{:S(2)}, u32[]{:S(2)}) async-start(bf16[64,2,256]{2,1,0:T(2,128)(2,1)} %reshape.4667), calls=%async_computation.5 | async-start | bytes 131072 | tf_op jit(solution)/shard_map/all_to_all | solution.py:178
  732.2 20.2 %all-to-all-start.3 = ((bf16[64,2,256]{2,1,0:T(2,128)(2,1)}), bf16[64,2,256]{2,1,0:T(2,128)(2,1)S(1)}, u32[]{:S(2)}, u32[]{:S(2)}) async-start(bf16[64,2,256]{2,1,0:T(2,128)(2,1)} %reshape.4663), calls=%async_computation.3 | async-start | bytes 131072 | tf_op jit(solution)/shard_map/all_to_all | solution.py:178
  752.4 19.4 %all-to-all-start.1 = ((bf16[64,2,256]{2,1,0:T(2,128)(2,1)}), bf16[64,2,256]{2,1,0:T(2,128)(2,1)S(1)}, u32[]{:S(2)}, u32[]{:S(2)}) async-start(bf16[64,2,256]{2,1,0:T(2,128)(2,1)} %reshape.4659), calls=%async_computation.1 | async-start | bytes 131072 | tf_op jit(solution)/shard_map/all_to_all | solution.py:178
  762.6 98.1 %all-gather.2.cloned.1.call-start = ((), (), s32[]{:S(2)}) async-start(), calls=%async_computation.12 | async-start | bytes 1966080 | tf_op jit(solution)/shard_map/all_gather | solution.py:203
  772.2 0.9 copy-start.2
  807.7 0.7 copy-start.1
Sparse Core Ops, SparseCore 0:
  817.3 43.3 all-gather.1
